TPU v7x, 512 devices: a whole 4x4x16 slice. The times are simulated.
512 devices in a mesh: rows: 64 (over y, z), cols: 8 (over x, core).
Axes of the slice: x: 4, y: 4, z: 16, core: 2. Of those that a mesh axis runs over, the one named last changes fastest.
Arguments:
- node_features: bfloat16 [65536, 512], P('rows', 'cols'), may hold values from -6 to 6
- weight: bfloat16 [512, 512], replicated, may hold values from -0.25 to 0.25
- tile_values: bfloat16 [4096, 128, 128], P('rows'), may hold values from -0.1875 to 0.1875
- tile_row: int32 [4096], P('rows'), may hold values from 0 to 7
- source_owner: int32 [4096, 1], P('rows'), may hold values from 0 to 63; in each aligned block of 64 rows (0 to 63, 64 to 127, ...) at most 2 rows name the same one
- source_block: int32 [4096], P('rows'), may hold values from 0 to 7
- labels: int32 [65536], P('rows'), may hold values from 0 to 511
Outputs:
- activations: bfloat16 [65536, 512], P('rows', 'cols')
- weight_grad: float32 [512, 512], P(None, 'cols')
- feature_grad: bfloat16 [65536, 512], P('rows', 'cols')
Inputs may be any that keep to these rules, and one draw needn't show every extreme that they name: `source_owner`: of the 64 tiles of one index of rows, at most 2 name the same owner.
All inputs are finite; a program needn't handle non-finite values.
Results may differ from a plain program's by a relative error of at most 0.0095.
Values may be sent and summed in bfloat16 or wider, within the bound.
A program may use at most 64 MiB of HBM per device.

v0:
```python
import math
import jax
import jax.numpy as jnp
from jax import lax
from jax.sharding import PartitionSpec as P


def slot_ranks(owners):
    positions = jnp.arange(owners.shape[0], dtype=jnp.int32)
    earlier = (owners[:, None] == owners[None, :]) & (positions[None, :] < positions[:, None])
    return jnp.sum(earlier.astype(jnp.int32), axis=1)


def per_device(node_features, weight, tile_values, tile_row, source_owner, source_block, labels):
    local_rows, col_width = node_features.shape
    block_size = tile_values.shape[1]
    local_blocks = local_rows // block_size
    row_devices = lax.axis_size("rows")
    capacity = 2 * tile_values.shape[0] // row_devices
    owners = source_owner[:, 0]
    slot_rank = slot_ranks(owners)
    column_block = owners * local_blocks + source_block
    local_ids = jnp.arange(local_blocks, dtype=jnp.int32)
    row_onehot = (tile_row[:, None] == local_ids[None, :]).astype(jnp.float32)
    gathered = lax.all_gather(node_features, "rows", axis=0, tiled=True)
    all_blocks = gathered.reshape(row_devices * local_blocks, block_size, col_width)
    source_rows = all_blocks[column_block]
    products = jnp.einsum(
        "tij,tjf->tif", tile_values, source_rows, preferred_element_type=jnp.float32
    )
    summed = jnp.einsum("tb,tif->bif", row_onehot, products, precision=lax.Precision.HIGHEST)
    aggregated = summed.reshape(local_rows, col_width).astype(jnp.bfloat16)
    aggregated_all = lax.all_gather(aggregated, "cols", axis=1, tiled=True)
    col_index = lax.axis_index("cols")
    w_columns = lax.dynamic_slice_in_dim(weight, col_index * col_width, col_width, 1)
    w_rows = lax.dynamic_slice_in_dim(weight, col_index * col_width, col_width, 0)
    hidden = jnp.dot(aggregated_all, w_columns, preferred_element_type=jnp.float32)
    sigmoid = jax.nn.sigmoid(hidden)
    activated = hidden * sigmoid
    slopes = sigmoid * (1.0 + hidden * (1.0 - sigmoid))
    feature_ids = col_index * col_width + jnp.arange(col_width, dtype=jnp.int32)
    target = (labels[:, None] == feature_ids[None, :]).astype(jnp.float32)
    out_grad = ((activated - target) * slopes).astype(jnp.bfloat16)
    grad_all = lax.all_gather(out_grad, "cols", axis=1, tiled=True)
    weight_terms = jnp.einsum(
        "nk,nc->kc", aggregated_all, out_grad, preferred_element_type=jnp.float32
    )
    node_total = local_rows * row_devices
    weight_grad = lax.psum(weight_terms, "rows") / math.sqrt(node_total)
    agg_grad = jnp.einsum("nc,kc->nk", grad_all, w_rows, preferred_element_type=jnp.float32).astype(
        jnp.bfloat16
    )
    grad_rows = agg_grad.reshape(local_blocks, block_size, col_width)[tile_row]
    sent_terms = jnp.einsum(
        "tji,tjf->tif", tile_values, grad_rows, preferred_element_type=jnp.float32
    )
    send_terms = (
        jnp.zeros((row_devices, capacity, block_size, col_width), jnp.float32)
        .at[owners, slot_rank]
        .set(sent_terms)
    )
    send_index = (
        jnp.zeros((row_devices, capacity), jnp.int32).at[owners, slot_rank].set(source_block)
    )
    received, recv_index = (
        lax.all_to_all(
            send_terms.astype(jnp.bfloat16), "rows", split_axis=0, concat_axis=0, tiled=True
        ).astype(send_terms.dtype),
        lax.all_to_all(send_index, "rows", split_axis=0, concat_axis=0, tiled=True),
    )
    placing = (recv_index[:, :, None] == local_ids[None, None, :]).astype(jnp.float32)
    filled = (jnp.abs(received).sum(axis=(2, 3)) >= 0.0).astype(jnp.float32)
    feature_grad = jnp.einsum(
        "scb,scif->bif", placing * filled[:, :, None], received, precision=lax.Precision.HIGHEST
    ).reshape(local_rows, col_width)
    return (activated.astype(jnp.bfloat16), weight_grad, feature_grad.astype(jnp.bfloat16))


def solution(mesh):
    return jax.shard_map(
        per_device,
        mesh=mesh,
        in_specs=(
            P("rows", "cols"),
            P(),
            P("rows", None, None),
            P("rows"),
            P("rows", None),
            P("rows"),
            P("rows"),
        ),
        out_specs=(P("rows", "cols"), P(None, "cols"), P("rows", "cols")),
        check_vma=False,
    )
```

profile of v0, /device:TPU:2, one launch (start us, length us, event | category | flops | bytes accessed | tf_op | source)
XLA Modules:
  0.0 590.2 jit_solution(7779311799218977783)
XLA Ops:
  8.6 164.2 %all-gather.4.cloned.1.call-done = bf16[65536,64]{0,1:T(8,128)(2,1)} async-done(((bf16[1024,64]{0,1:T(8,128)(2,1)}), bf16[65536,64]{0,1:T(8,128)(2,1)}) %all-gather.4.cloned.1.call-update) | async-done | bytes 8388624 | tf_op jit(solution)/shard_map/all_gather | solution.py:25
  172.9 9.0 %copy_bitcast_fusion = bf16[512,128,64]{1,2,0:T(8,128)(2,1)} fusion(bf16[65536,64]{0,1:T(8,128)(2,1)} %all-gather.4.cloned.1.call-done), kind=kLoop, calls=%fused_computation.4 | loop fusion | bytes 16777216 | tf_op jit(solution)/shard_map/reshape | solution.py:26
  181.9 4.1 gather_fusion
  186.0 1.5 convolution_bitcast_fusion.1
  187.6 2.0 fusion.10
  190.4 24.7 %all-gather.6.cloned.1.call-done = bf16[1024,512]{0,1:T(8,128)(2,1)} async-done(((bf16[1024,64]{0,1:T(8,128)(2,1)}), bf16[1024,512]{0,1:T(8,128)(2,1)}) %all-gather.6.cloned.1.call-update) | async-done | bytes 1048592 | tf_op jit(solution)/shard_map/all_gather | solution.py:33
  215.0 2.4 multiply_convert_fusion
  217.7 3.5 scatter_fusion
  221.2 0.7 copy.42
  221.9 15.2 %all-to-all-start = ((s32[64,1,2]{2,1,0:T(1,128)}), s32[64,1,2]{2,1,0:T(1,128)S(1)}, u32[]{:S(2)}, u32[]{:S(2)}) async-start(s32[64,1,2]{2,1,0:T(1,128)} %copy.42), calls=%async_computation | async-start | bytes 65536 | tf_op jit(solution)/shard_map/all_to_all | solution.py:69
  237.1 11.6 %all-gather.8.cloned.1.call-done = bf16[1024,512]{0,1:T(8,128)(2,1)} async-done(((bf16[1024,64]{0,1:T(8,128)(2,1)}), bf16[1024,512]{0,1:T(8,128)(2,1)}) %all-gather.8.cloned.1.call-update) | async-done | bytes 1048592 | tf_op jit(solution)/shard_map/all_gather | solution.py:44
  248.7 1.6 fusion.13
  250.3 0.8 gather_fusion.1
  251.1 2.0 convolution_bitcast_fusion
  253.1 2.5 broadcast_in_dim.10
  255.6 10.6 %scatter_fusion.1 = f32[64,2,128,64]{2,3,1,0:T(8,128)} fusion(f32[64,2,128,64]{2,3,1,0:T(8,128)} %broadcast_in_dim.10, s32[64]{0:T(128)S(1)} %fusion.31, f32[64,128,64]{1,2,0:T(8,128)} %convolution_bitcast_fusion), kind=kCustom, calls=%fused_computation.3 | custom fusion | bytes 6291968 | tf_op jit(solution)/shard_map/scatter | solution.py:60
  266.2 2.7 convert_element_type.49
  268.9 3.5 copy.45
  272.4 15.9 %all-to-all-start.1 = ((bf16[64,2,128,64]{2,1,3,0:T(2,128)(2,1)}), bf16[64,2,128,64]{2,1,3,0:T(2,128)(2,1)}, u32[]{:S(2)}, u32[]{:S(2)}) async-start(bf16[64,2,128,64]{2,1,3,0:T(2,128)(2,1)} %copy.45), calls=%async_computation.1 | async-start | bytes 4194304 | tf_op jit(solution)/shard_map/all_to_all | solution.py:66
  288.4 1.1 fusion.33
  289.6 283.3 %all-reduce.2.cloned.1.call-done = f32[512,64]{0,1:T(8,128)} async-done(((f32[512,64]{0,1:T(8,128)}), f32[512,64]{0,1:T(8,128)}) %all-reduce.2.cloned.1.call-update) | async-done | bytes 131088 | tf_op jit(solution)/shard_map/psum | solution.py:49
  573.0 1.6 broadcast_multiply_fusion
  574.5 3.8 abs_reduce_fusion
  578.5 4.5 fusion.7
  (38 shorter events, 3.4 us)
Async XLA Ops:
  7.2 178.9 %copy-start = (bf16[64,128,128]{2,1,0:T(8,128)(2,1)S(1)}, bf16[64,128,128]{2,1,0:T(8,128)(2,1)}, u32[]{:S(2)}) copy-start(bf16[64,128,128]{2,1,0:T(8,128)(2,1)} %param.9) | copy-start | bytes 6291460
  7.2 165.7 %all-gather.4.cloned.1.call-start = ((), (), s32[]{:S(2)}) async-start(), calls=%async_computation.2 | async-start | bytes 8519680 | tf_op jit(solution)/shard_map/all_gather | solution.py:25
  7.9 207.1 %all-gather.6.cloned.1.call-start = ((), (), s32[]{:S(2)}) async-start(), calls=%async_computation.3 | async-start | bytes 1179648 | tf_op jit(solution)/shard_map/all_gather | solution.py:33
  186.0 1.5 copy-start.4
  187.6 27.4 %copy-start.5 = (s32[1024]{0:T(1024)S(1)}, s32[1024]{0:T(1024)}, u32[]{:S(2)}) copy-start(s32[1024]{0:T(1024)} %param.13) | copy-start | bytes 12292
  189.6 27.9 %copy-start.6 = (s32[64,1]{0,1:T(1,128)S(1)}, s32[64,1]{0,1:T(1,128)}, u32[]{:S(2)}) copy-start(s32[64,1]{0,1:T(1,128)} %param.11) | copy-start | bytes 772
  189.6 28.1 %copy-start.3 = (s32[64]{0:T(128)S(1)}, s32[64]{0:T(128)}, u32[]{:S(2)}) copy-start(s32[64]{0:T(128)} %param.12) | copy-start | bytes 772
  190.3 58.4 %all-gather.8.cloned.1.call-start = ((), (), s32[]{:S(2)}) async-start(), calls=%async_computation.5 | async-start | bytes 1179648 | tf_op jit(solution)/shard_map/all_gather | solution.py:44
  221.9 50.5 %all-to-all-start = ((s32[64,1,2]{2,1,0:T(1,128)}), s32[64,1,2]{2,1,0:T(1,128)S(1)}, u32[]{:S(2)}, u32[]{:S(2)}) async-start(s32[64,1,2]{2,1,0:T(1,128)} %copy.42), calls=%async_computation | async-start | bytes 65536 | tf_op jit(solution)/shard_map/all_to_all | solution.py:69
  272.4 16.0 %copy-start.1 = (bf16[1024,512]{0,1:T(8,128)(2,1)S(1)}, bf16[1024,512]{0,1:T(8,128)(2,1)}, u32[]{:S(2)}) copy-start(bf16[1024,512]{0,1:T(8,128)(2,1)} %all-gather.6.cloned.1.call-done) | copy-start | bytes 3145732
  272.4 16.0 %copy-start.2 = (bf16[1024,64]{0,1:T(8,128)(2,1)S(1)}, bf16[1024,64]{0,1:T(8,128)(2,1)}, u32[]{:S(2)}) copy-start(bf16[1024,64]{0,1:T(8,128)(2,1)} %get-tuple-element.3) | copy-start | bytes 393220
  272.4 302.1 %all-to-all-start.1 = ((bf16[64,2,128,64]{2,1,3,0:T(2,128)(2,1)}), bf16[64,2,128,64]{2,1,3,0:T(2,128)(2,1)}, u32[]{:S(2)}, u32[]{:S(2)}) async-start(bf16[64,2,128,64]{2,1,3,0:T(2,128)(2,1)} %copy.45), calls=%async_computation.1 | async-start | bytes 4194304 | tf_op jit(solution)/shard_map/all_to_all | solution.py:66
  288.4 284.6 %all-reduce.2.cloned.1.call-start = ((), (), s32[]{:S(2)}) async-start(), calls=%async_computation.4 | async-start | bytes 262144 | tf_op jit(solution)/shard_map/psum | solution.py:49
Sparse Core Ops, SparseCore 0:
  11.0 161.8 all-gather.3
  190.4 24.5 all-gather.5
  217.7 30.9 all-gather.7
  292.9 280.0 all-reduce.1
where the time goes:
time: 591 us; the launch traced here: 590 us
  waiting for transfers between devices  485 us (82%)
  local copies, waits for them, and re-layouts  36.3 us (6%)
  starting transfers between devices  31.3 us (5%)
  matrix products  15.1 us (3%)
  between operations  14 us (2%)
  other arithmetic  9.01 us (2%)
    psum x1, waiting for transfers between devices, per_device(): weight_grad = lax.psum(weight_terms, 'rows') / math.sqrt(node_total)  283 us
    all_gather x1, waiting for transfers between devices, per_device(): gathered = lax.all_gather(node_features, 'rows', axis=0, tiled=True)  164 us
    all_gather x1, waiting for transfers between devices, per_device(): aggregated_all = lax.all_gather(aggregated, 'cols', axis=1, tiled=True)  24.7 us
    all_to_all x1, starting transfers between devices, per_device(): lax.all_to_all(send_terms.astype(jnp.bfloat16), 'rows', split_axis=0, con...  15.9 us
    all_to_all x1, starting transfers between devices, per_device(): lax.all_to_all(send_index, 'rows', split_axis=0, concat_axis=0, tiled=True)  15.2 us
  transfers between devices with their start and end apart: 6, of which 4 were waited for; matrix products, arithmetic and copies ran while one was open for 5% of the time, Pallas kernels for 0%

commit v1 on v0

--- a/solution.py
+++ b/solution.py
@@ -46,7 +46,7 @@
         "nk,nc->kc", aggregated_all, out_grad, preferred_element_type=jnp.float32
     )
     node_total = local_rows * row_devices
-    weight_grad = lax.psum(weight_terms, "rows") / math.sqrt(node_total)
+    weight_grad = jnp.sum(lax.all_gather(weight_terms, "rows"), axis=0) / math.sqrt(node_total)
     agg_grad = jnp.einsum("nc,kc->nk", grad_all, w_rows, preferred_element_type=jnp.float32).astype(
         jnp.bfloat16
     )

time: 591 us -> 464 us (0.79)
  the two profiles are of different devices: /device:TPU:2 before, /device:TPU:8 now
where the time goes in v1:
time: 464 us
  waiting for transfers between devices  346 us (75%)
  local copies, waits for them, and re-layouts  44.6 us (10%)
  starting transfers between devices  31.9 us (7%)
  matrix products  16.1 us (3%)
  between operations  14 us (3%)
  other arithmetic  10.5 us (2%)
    all_gather x1, waiting for transfers between devices, per_device(): gathered = lax.all_gather(node_features, 'rows', axis=0, tiled=True)  163 us
    all_to_all x1, waiting for transfers between devices, per_device(): lax.all_to_all(send_terms.astype(jnp.bfloat16), 'rows', split_axis=0, con...  106 us
    all_gather x1, waiting for transfers between devices, per_device(): lax.all_gather(weight_terms, 'rows')  40.4 us
    all_gather x1, waiting for transfers between devices, per_device(): aggregated_all = lax.all_gather(aggregated, 'cols', axis=1, tiled=True)  27.1 us
    all_to_all x1, starting transfers between devices, per_device(): lax.all_to_all(send_terms.astype(jnp.bfloat16), 'rows', split_axis=0, con...  16 us
    all_to_all x1, starting transfers between devices, per_device(): lax.all_to_all(send_index, 'rows', split_axis=0, concat_axis=0, tiled=True)  15.7 us
    scatter x1, local copies, waits for them, and re-layouts, per_device(): send_terms = jnp.zeros((row_devices, capacity, block_size, col_width), jn...  10.7 us
    unnamed x15, local copies, waits for them, and re-layouts  9.52 us
  transfers between devices with their start and end apart: 6, of which 5 were waited for; matrix products, arithmetic and copies ran while one was open for 9% of the time, Pallas kernels for 0%

profile of v1, /device:TPU:8, one launch (start us, length us, event | category | flops | bytes accessed | tf_op | source)
XLA Modules:
  0.0 463.5 jit_solution(2257676838799061647)
XLA Ops:
  8.6 162.9 %all-gather.6.cloned.1.call-done = bf16[65536,64]{0,1:T(8,128)(2,1)} async-done(((bf16[1024,64]{0,1:T(8,128)(2,1)}), bf16[65536,64]{0,1:T(8,128)(2,1)}) %all-gather.6.cloned.1.call-update) | async-done | bytes 8388624 | tf_op jit(solution)/shard_map/all_gather | solution.py:25
  171.6 9.0 %copy_bitcast_fusion = bf16[512,128,64]{1,2,0:T(8,128)(2,1)} fusion(bf16[65536,64]{0,1:T(8,128)(2,1)} %all-gather.6.cloned.1.call-done), kind=kLoop, calls=%fused_computation.5 | loop fusion | bytes 16777216 | tf_op jit(solution)/shard_map/reshape | solution.py:26
  180.6 4.1 gather_fusion
  184.8 1.5 convolution_bitcast_fusion.1
  186.3 2.0 fusion.10
  189.1 27.1 %all-gather.8.cloned.1.call-done = bf16[1024,512]{0,1:T(8,128)(2,1)} async-done(((bf16[1024,64]{0,1:T(8,128)(2,1)}), bf16[1024,512]{0,1:T(8,128)(2,1)}) %all-gather.8.cloned.1.call-update) | async-done | bytes 1048592 | tf_op jit(solution)/shard_map/all_gather | solution.py:33
  216.1 2.5 multiply_convert_fusion
  218.7 2.0 fusion.33
  221.0 3.5 scatter_fusion
  225.2 15.7 %all-to-all-start = ((s32[64,1,2]{2,1,0:T(1,128)}), s32[64,1,2]{2,1,0:T(1,128)S(1)}, u32[]{:S(2)}, u32[]{:S(2)}) async-start(s32[64,1,2]{2,1,0:T(1,128)} %copy.42), calls=%async_computation | async-start | bytes 65536 | tf_op jit(solution)/shard_map/all_to_all | solution.py:69
  240.9 8.9 %all-gather.10.cloned.1.call-done = bf16[1024,512]{0,1:T(8,128)(2,1)} async-done(((bf16[1024,64]{0,1:T(8,128)(2,1)}), bf16[1024,512]{0,1:T(8,128)(2,1)}) %all-gather.10.cloned.1.call-update) | async-done | bytes 1048592 | tf_op jit(solution)/shard_map/all_gather | solution.py:44
  249.9 1.6 fusion.13
  252.2 2.0 convolution_bitcast_fusion
  254.2 2.5 broadcast_in_dim.10
  256.7 10.7 %scatter_fusion.1 = f32[64,2,128,64]{2,3,1,0:T(8,128)} fusion(f32[64,2,128,64]{2,3,1,0:T(8,128)} %broadcast_in_dim.10, s32[64]{0:T(128)S(1)} %fusion.31, f32[64,128,64]{1,2,0:T(8,128)} %convolution_bitcast_fusion), kind=kCustom, calls=%fused_computation.3 | custom fusion | bytes 6291968 | tf_op jit(solution)/shard_map/scatter | solution.py:60
  267.5 2.7 convert_element_type.49
  270.2 3.5 copy.45
  273.7 16.0 %all-to-all-start.1 = ((bf16[64,2,128,64]{2,1,3,0:T(2,128)(2,1)}), bf16[64,2,128,64]{2,1,3,0:T(2,128)(2,1)}, u32[]{:S(2)}, u32[]{:S(2)}) async-start(bf16[64,2,128,64]{2,1,3,0:T(2,128)(2,1)} %copy.45), calls=%async_computation.1 | async-start | bytes 4194304 | tf_op jit(solution)/shard_map/all_to_all | solution.py:66
  289.7 106.5 %all-to-all-done.1 = bf16[64,2,128,64]{2,1,3,0:T(2,128)(2,1)} async-done(((bf16[64,2,128,64]{2,1,3,0:T(2,128)(2,1)}), bf16[64,2,128,64]{2,1,3,0:T(2,128)(2,1)}, u32[]{:S(2)}, u32[]{:S(2)}) %all-to-all-start.1) | async-done | bytes 2097184 | tf_op jit(solution)/shard_map/all_to_all | solution.py:66
  396.2 3.9 abs_reduce_fusion
  400.2 4.6 fusion.7
  405.4 40.4 %all-gather.12.cloned.1.call-done = f32[32768,64]{0,1:T(8,128)} async-done(((f32[512,64]{0,1:T(8,128)}), f32[32768,64]{0,1:T(8,128)}) %all-gather.12.cloned.1.call-update) | async-done | bytes 8388624 | tf_op jit(solution)/shard_map/all_gather | solution.py:49
  445.8 8.1 %copy.52 = f32[8,8,64,512]{3,2,1,0:T(8,128)S(1)} copy(f32[8,8,64,512]{3,1,2,0:T(8,128)} %bitcast.62) | data formatting | bytes 16777216
  453.9 2.4 bitcast_reduce_fusion
  (38 shorter events, 5.5 us)
Async XLA Ops:
  7.2 177.6 %copy-start = (bf16[64,128,128]{2,1,0:T(8,128)(2,1)S(1)}, bf16[64,128,128]{2,1,0:T(8,128)(2,1)}, u32[]{:S(2)}) copy-start(bf16[64,128,128]{2,1,0:T(8,128)(2,1)} %param.9) | copy-start | bytes 6291460
  7.2 164.4 %all-gather.6.cloned.1.call-start = ((), (), s32[]{:S(2)}) async-start(), calls=%async_computation.2 | async-start | bytes 8519680 | tf_op jit(solution)/shard_map/all_gather | solution.py:25
  7.9 208.2 %all-gather.8.cloned.1.call-start = ((), (), s32[]{:S(2)}) async-start(), calls=%async_computation.3 | async-start | bytes 1179648 | tf_op jit(solution)/shard_map/all_gather | solution.py:33
  184.8 1.5 copy-start.3
  186.3 29.8 %copy-start.4 = (s32[1024]{0:T(1024)S(1)}, s32[1024]{0:T(1024)}, u32[]{:S(2)}) copy-start(s32[1024]{0:T(1024)} %param.13) | copy-start | bytes 12292
  189.0 60.9 %all-gather.10.cloned.1.call-start = ((), (), s32[]{:S(2)}) async-start(), calls=%async_computation.4 | async-start | bytes 1179648 | tf_op jit(solution)/shard_map/all_gather | solution.py:44
  189.0 31.7 %copy-start.5 = (s32[64,1]{0,1:T(1,128)S(1)}, s32[64,1]{0,1:T(1,128)}, u32[]{:S(2)}) copy-start(s32[64,1]{0,1:T(1,128)} %param.11) | copy-start | bytes 772
  189.1 31.9 %copy-start.2 = (s32[64]{0:T(128)S(1)}, s32[64]{0:T(128)}, u32[]{:S(2)}) copy-start(s32[64]{0:T(128)} %param.12) | copy-start | bytes 772
  216.1 2.6 copy-start.1
  218.7 227.1 %all-gather.12.cloned.1.call-start = ((), (), s32[]{:S(2)}) async-start(), calls=%async_computation.5 | async-start | bytes 8519680 | tf_op jit(solution)/shard_map/all_gather | solution.py:49
  225.2 48.5 %all-to-all-start = ((s32[64,1,2]{2,1,0:T(1,128)}), s32[64,1,2]{2,1,0:T(1,128)S(1)}, u32[]{:S(2)}, u32[]{:S(2)}) async-start(s32[64,1,2]{2,1,0:T(1,128)} %copy.42), calls=%async_computation | async-start | bytes 65536 | tf_op jit(solution)/shard_map/all_to_all | solution.py:69
  273.7 122.5 %all-to-all-start.1 = ((bf16[64,2,128,64]{2,1,3,0:T(2,128)(2,1)}), bf16[64,2,128,64]{2,1,3,0:T(2,128)(2,1)}, u32[]{:S(2)}, u32[]{:S(2)}) async-start(bf16[64,2,128,64]{2,1,3,0:T(2,128)(2,1)} %copy.45), calls=%async_computation.1 | async-start | bytes 4194304 | tf_op jit(solution)/shard_map/all_to_all | solution.py:66
Sparse Core Ops, SparseCore 0:
  11.0 160.5 all-gather.5
  189.1 26.9 all-gather.7
  218.9 30.9 all-gather.9
  253.2 192.4 all-gather.11
